TPU v7x, 128 devices: a whole 4x4x4 slice. The times are simulated.
128 devices in a mesh: frag: 4 (over y_hi, core), aux: 16 (over z, x), orb: 2 (over y_lo).
Axes of the slice: x: 4, y: 4 (y_hi: 2, y_lo: 2; y = y_hi * 2 + y_lo), z: 4, core: 2. Of those that a mesh axis runs over, the one named last changes fastest.
Arguments:
- density: bfloat16 [16384, 2, 8192], P('frag', 'orb', 'aux'), may hold values from -0.046875 to 0.046875
- bath: bfloat16 [16, 2, 8192, 128], P('frag', 'orb', 'aux'), may hold values from -1 to 1
- factor: bfloat16 [16384, 16384], P('orb', 'aux'), may hold values from -6 to 6
- frag_index: int32 [16, 128], replicated, may hold values from 0 to 16383, as said below
- nfrag: int32 [16], replicated, may hold values from 1 to 128
- nbath: int32 [16], replicated, may hold values from 1 to 128
Outputs:
- projected: bfloat16 [16, 256, 16384], P('frag', 'orb', 'aux')
Inputs may be any that keep to these rules, and one draw needn't show every extreme that they name: `frag_index`: the 128 entries of one fragment's row are distinct basis functions; entries at or past nfrag are not read.
All inputs are finite; a program needn't handle non-finite values.
Results may differ from a plain program's by a relative error of at most 0.0049.
Values may be sent and summed in bfloat16 or wider, within the bound.
A program may use at most 128 MiB of HBM per device.

v0:
```python
import jax
import jax.numpy as jnp
from jax import lax
from jax.sharding import PartitionSpec as P


def per_device(density, bath, factor, frag_index, nfrag, nbath):
    local_rows = density.shape[0]
    block_cols = density.shape[2]
    density_local = density.reshape(local_rows, block_cols)
    group_size = bath.shape[0]
    frag_max = frag_index.shape[1]
    bath_max = bath.shape[3]
    frag_count = frag_index.shape[0]
    row_offset = lax.axis_index("frag") * local_rows
    local_index = frag_index - row_offset
    owned_rows = (local_index >= 0) & (local_index < local_rows)
    picked = jnp.take(density_local, jnp.clip(local_index, 0, local_rows - 1).reshape(-1), axis=0)
    picked = picked.reshape(frag_count, frag_max, block_cols)
    picked = jnp.where(owned_rows[:, :, None], picked, jnp.zeros_like(picked))
    gathered_rows = (
        lax.psum_scatter(picked, "frag", scatter_dimension=0, tiled=True)
        .astype(jnp.float32)
        .astype(jnp.bfloat16)
    )
    first_frag = lax.axis_index("frag") * group_size
    my_nfrag = lax.dynamic_slice_in_dim(nfrag, first_frag, group_size)
    my_nbath = lax.dynamic_slice_in_dim(nbath, first_frag, group_size)
    frag_live = jnp.arange(frag_max, dtype=jnp.int32)[None, :] < my_nfrag[:, None]
    bath_live = jnp.arange(bath_max, dtype=jnp.int32)[None, :] < my_nbath[:, None]
    gathered_rows = jnp.where(frag_live[:, :, None], gathered_rows, jnp.zeros_like(gathered_rows))
    bath_cols = bath.reshape(group_size, block_cols, bath_max)
    bath_cols = jnp.where(bath_live[:, None, :], bath_cols, jnp.zeros_like(bath_cols))
    initial = jnp.concatenate([jnp.swapaxes(gathered_rows, 1, 2), bath_cols], axis=2)
    live_cols = jnp.concatenate([frag_live, bath_live], axis=1).astype(jnp.float32)
    kmax_cols = initial.shape[2]
    identity_pad = jnp.eye(kmax_cols, dtype=jnp.float32)[None] * (1.0 - live_cols)[:, :, None]
    gram_part = jnp.einsum("fmk,fml->fkl", initial, initial, preferred_element_type=jnp.float32)
    gram_total = lax.psum(gram_part, ("aux", "orb")) + identity_pad
    cholesky_low = jnp.linalg.cholesky(gram_total)
    coeffs = lax.linalg.triangular_solve(
        cholesky_low, initial.astype(jnp.float32), left_side=False, lower=True, transpose_a=True
    )
    coeffs = coeffs.astype(jnp.bfloat16)
    partial_value = jnp.einsum(
        "fmk,mq->fkq",
        lax.all_gather(coeffs, "aux", axis=1, tiled=True),
        factor,
        preferred_element_type=jnp.float32,
    )
    summed = lax.psum_scatter(partial_value, "orb", scatter_dimension=1, tiled=True)
    return summed.astype(jnp.bfloat16)


def solution(mesh):
    placed = (
        P("frag", "orb", "aux"),
        P("frag", "orb", "aux", None),
        P("orb", "aux"),
        P(),
        P(),
        P(),
    )
    return jax.shard_map(
        per_device, mesh=mesh, in_specs=placed, out_specs=P("frag", "orb", "aux"), check_vma=False
    )
```

profile of v0, /device:TPU:1, one launch (start us, length us, event | category | flops | bytes accessed | tf_op | source)
XLA Modules:
  0.0 812.8 jit_solution(12678690382864565310)
XLA Ops:
  6.5 0.0 reduce-scatter.3.cloned.1.call-start
  6.5 0.7 compare_and_fusion
  7.3 10.3 %gather_fusion = bf16[2048,512]{1,0:T(8,128)(2,1)S(1)} fusion(bf16[4096,512]{1,0:T(8,128)(2,1)} %bitcast.50, s32[2048]{0:T(1024)S(1)} %broadcast_clamp_fusion), kind=kCustom, calls=%fused_computation | custom fusion | bytes 4202496 | tf_op jit(solution)/shard_map/jit(_take)/gather | solution.py:18
  17.6 2.4 copy.24
  20.0 3.2 select_select_fusion
  23.2 0.0 copy-start.5
  23.2 0.0 copy-start.6
  23.2 0.0 copy-start.4
  23.2 0.0 reduce-scatter.3.cloned.1.call-update
  23.2 0.0 all-reduce.3.cloned.1.call-start
  23.3 0.6 copy-done.5
  23.8 0.1 dynamic_slice.6
  23.9 0.0 copy-done.6
  23.9 0.1 dynamic_slice.7
  24.0 0.1 iota_compare_fusion.4
  24.1 0.2 copy-done.4
  24.3 0.0 copy-start.2
  24.3 40.2 %reduce-scatter.3.cloned.1.call-done = bf16[4,128,512]{1,2,0:T(8,128)(2,1)} async-done(((bf16[16,128,512]{1,2,0:T(8,128)(2,1)}), bf16[4,128,512]{1,2,0:T(8,128)(2,1)}) %reduce-scatter.3.cloned.1.call-update) | async-done | bytes 524304 | tf_op jit(solution)/shard_map/reduce_scatter | solution.py:22
  64.5 1.1 fusion.8
  65.6 1.5 fusion.2
  67.1 0.0 all-reduce.3.cloned.1.call-update
  67.1 0.0 copy-done.2
  67.1 0.2 all-gather.2.cloned.1.call-start
  67.5 286.9 %all-reduce.3.cloned.1.call-done = f32[4,256,256]{1,2,0:T(8,128)} async-done(((f32[4,256,256]{1,2,0:T(8,128)}), f32[4,256,256]{1,2,0:T(8,128)}) %all-reduce.3.cloned.1.call-update) | async-done | bytes 1048592 | tf_op jit(solution)/shard_map/psum | solution.py:39
  354.4 0.0 copy-start
  354.4 1.4 multiply_add_fusion
  355.9 0.3 copy.27
  356.2 0.0 copy-done
  356.2 0.2 fusion.6
  356.4 46.9 %custom-call.16 = f32[4,128,128]{2,1,0:T(8,128)S(1)} custom-call(f32[4,128,128]{2,1,0:T(8,128)S(1)} %cholesky.122), custom_call_target="Cholesky" | custom-call | tf_op jit(solution)/shard_map/jit(cholesky)/cholesky | solution.py:40
  403.3 39.3 %custom-call.17 = f32[4,1,128,128]{2,3,1,0:T(8,128)S(1)} custom-call(f32[4,1,128,128]{3,2,1,0:T(8,128)S(1)} %select_bitcast_fusion), custom_call_target="InvertDiagBlocksLowerTriangular" | custom-call | tf_op jit(solution)/shard_map/jit(cholesky)/cholesky | solution.py:40
  442.6 0.1 cholesky.117
  442.7 0.4 constant_dynamic-update-slice_fusion.1
  443.1 0.7 convolution_subtract_fusion.1
  443.8 46.9 %custom-call.18 = f32[4,128,128]{2,1,0:T(8,128)S(1)} custom-call(f32[4,128,128]{2,1,0:T(8,128)S(1)} %convolution_subtract_fusion.1), custom_call_target="Cholesky" | custom-call | tf_op jit(solution)/shard_map/jit(cholesky)/cholesky | solution.py:40
  490.7 0.1 select_reduce_fusion
  490.8 0.1 compare_reduce_fusion
  490.9 0.1 compare_reduce_fusion.1
  491.0 0.0 copy-start.1
  491.0 0.2 select_select_fusion.1
  491.2 0.1 triangular_solve.63
  491.3 0.0 copy-start.3
  491.3 5.4 while.1
  491.3 0.6 fusion.25
  491.9 2.1 bitcast_dynamic-update-slice_fusion.2
  494.0 0.6 fusion.25
  494.6 2.1 bitcast_dynamic-update-slice_fusion.2
  496.7 79.4 %custom-call.19 = f32[4,2,128,128]{2,3,1,0:T(8,128)S(1)} custom-call(f32[4,2,128,128]{3,2,1,0:T(8,128)} %bitcast.54), custom_call_target="InvertDiagBlocksLowerTriangular" | custom-call | tf_op jit(solution)/shard_map/triangular_solve | solution.py:41
  576.1 0.0 copy-done.1
  576.1 0.6 fusion.18
  576.8 0.0 copy-done.3
  576.8 1.8 convolution_subtract_fusion
  578.6 1.1 convolution_convert_fusion
  579.7 1.0 pad_maximum_fusion
  580.7 0.0 all-gather.2.cloned.1.call-update
  580.7 0.0 reduce-scatter.5.cloned.1.call-start
  580.8 141.7 %all-gather.2.cloned.1.call-done = bf16[4,8192,256]{1,2,0:T(8,128)(2,1)} async-done(((bf16[4,512,256]{1,2,0:T(8,128)(2,1)}), bf16[4,8192,256]{1,2,0:T(8,128)(2,1)}) %all-gather.2.cloned.1.call-update) | async-done | bytes 16777232 | tf_op jit(solution)/shard_map/all_gather | solution.py:47
  722.5 23.5 %fusion = f32[4,256,1024]{2,1,0:T(8,128)} fusion(bf16[4,8192,256]{1,2,0:T(8,128)(2,1)} %all-gather.2.cloned.1.call-done, bf16[8192,1024]{1,0:T(8,128)(2,1)} %param.8), kind=kOutput, calls=%fused_computation.3 | convolution fusion | flops 17179869184 | bytes 37748736 | tf_op jit(solution)/shard_map/fmk,mq->fkq/dot_general | solution.py:45
  746.0 0.0 reduce-scatter.5.cloned.1.call-update
  746.0 57.5 %reduce-scatter.5.cloned.1.call-done = f32[4,128,1024]{2,1,0:T(8,128)} async-done(((f32[4,256,1024]{2,1,0:T(8,128)}), f32[4,128,1024]{2,1,0:T(8,128)}) %reduce-scatter.5.cloned.1.call-update) | async-done | bytes 2097168 | tf_op jit(solution)/shard_map/reduce_scatter | solution.py:51
  803.5 2.7 convert_element_type.23
  (15 shorter events, 0.2 us)
Async XLA Ops:
  6.5 58.0 %reduce-scatter.3.cloned.1.call-start = ((), (), s32[]{:S(2)}) async-start(), calls=%async_computation.2 | async-start | bytes 2621440 | tf_op jit(solution)/shard_map/reduce_scatter | solution.py:22
  23.2 0.7 copy-start.5
  23.2 0.7 copy-start.6
  23.2 1.1 copy-start.4
  23.2 331.2 %all-reduce.3.cloned.1.call-start = ((), (), s32[]{:S(2)}) async-start(), calls=%async_computation.3 | async-start | bytes 2097152 | tf_op jit(solution)/shard_map/psum | solution.py:39
  24.3 42.8 %copy-start.2 = (bf16[4,512,128]{2,1,0:T(8,128)(2,1)}, bf16[4,512,128]{2,1,0:T(8,128)(2,1)S(1)}, u32[]{:S(2)}) copy-start(bf16[4,512,128]{2,1,0:T(8,128)(2,1)S(1)} %bitcast_select_fusion) | copy-start | bytes 1572868
  67.1 655.4 %all-gather.2.cloned.1.call-start = ((), (), s32[]{:S(2)}) async-start(), calls=%async_computation.4 | async-start | bytes 17825792 | tf_op jit(solution)/shard_map/all_gather | solution.py:47
  354.4 1.8 copy-start
  491.0 85.1 %copy-start.1 = (bf16[4,128,512]{1,2,0:T(8,128)(2,1)S(1)}, bf16[4,128,512]{1,2,0:T(8,128)(2,1)}, u32[]{:S(2)}) copy-start(bf16[4,128,512]{1,2,0:T(8,128)(2,1)} %reduce-scatter.3.cloned.1.call-done) | copy-start | bytes 1572868
  491.3 85.5 %copy-start.3 = (bf16[4,512,128]{2,1,0:T(8,128)(2,1)S(1)}, bf16[4,512,128]{2,1,0:T(8,128)(2,1)}, u32[]{:S(2)}) copy-start(bf16[4,512,128]{2,1,0:T(8,128)(2,1)} %copy-done.2) | copy-start | bytes 1572868
  580.7 222.8 %reduce-scatter.5.cloned.1.call-start = ((), (), s32[]{:S(2)}) async-start(), calls=%async_computation.5 | async-start | bytes 6291456 | tf_op jit(solution)/shard_map/reduce_scatter | solution.py:51
Sparse Core Ops, SparseCore 0:
  23.3 41.1 reduce-scatter.2
  67.2 287.1 all-reduce.2
  580.9 141.6 all-gather.1
  746.2 57.3 reduce-scatter.4
where the time goes:
time: 813 us
  waiting for transfers between devices  526 us (65%)
  other arithmetic  224 us (28%)
  matrix products  29.6 us (4%)
  local copies, waits for them, and re-layouts  19.5 us (2%)
  between operations  13.4 us (2%)
    psum x1, waiting for transfers between devices, per_device(): gram_total = lax.psum(gram_part, ('aux', 'orb')) + identity_pad  287 us
    all_gather x1, waiting for transfers between devices, per_device(): lax.all_gather(coeffs, 'aux', axis=1, tiled=True)  142 us
    another operation x10, other arithmetic, per_device(): cholesky_low = jnp.linalg.cholesky(gram_total)  133 us
    another operation x5, other arithmetic, per_device(): lax.linalg.triangular_solve(cholesky_low, initial.astype(jnp.float32), le...  80.7 us
    reduce_scatter x1, waiting for transfers between devices, per_device(): lax.psum_scatter(partial_value, 'orb', scatter_dimension=1, tiled=True)  57.5 us
    reduce_scatter x1, waiting for transfers between devices, per_device(): lax.psum_scatter(picked, 'frag', scatter_dimension=0, tiled=True)  40.2 us
    dot_general x1, matrix products, per_device(): jnp.einsum('fmk,mq->fkq', lax.all_gather(coeffs, 'aux', axis=1, tiled=Tru...  23.5 us
  transfers between devices with their start and end apart: 4, of which 4 were waited for; matrix products, arithmetic and copies ran while one was open for 0% of the time, Pallas kernels for 0%

commit v1 on v0

--- a/solution.py
+++ b/solution.py
@@ -36,7 +36,7 @@
     kmax_cols = initial.shape[2]
     identity_pad = jnp.eye(kmax_cols, dtype=jnp.float32)[None] * (1.0 - live_cols)[:, :, None]
     gram_part = jnp.einsum("fmk,fml->fkl", initial, initial, preferred_element_type=jnp.float32)
-    gram_total = lax.psum(gram_part, ("aux", "orb")) + identity_pad
+    gram_total = lax.psum(lax.psum(gram_part, "aux"), "orb") + identity_pad
     cholesky_low = jnp.linalg.cholesky(gram_total)
     coeffs = lax.linalg.triangular_solve(
         cholesky_low, initial.astype(jnp.float32), left_side=False, lower=True, transpose_a=True

time: 813 us -> 640 us (0.79)
  waiting for transfers between devices: 526 us -> 353 us
    psum x1 -> x2, waiting for transfers between devices: 287 us -> 135 us  [per_device(): gram_total = lax.psum(lax.psum(gram_part, 'aux'), 'orb') + identity_pad]
    all_gather x1, waiting for transfers between devices: 142 us -> 120 us  [per_device(): lax.all_gather(coeffs, 'aux', axis=1, tiled=True)]
  transfers between devices with their start and end apart: 4 -> 5, of which waited for: 4 -> 5; matrix products, arithmetic and copies ran while one was open for 0% -> 0% of each run, Pallas kernels for 0% -> 0%
where the time goes in v1:
time: 640 us
  waiting for transfers between devices  353 us (55%)
  other arithmetic  224 us (35%)
  matrix products  29.6 us (5%)
  local copies, waits for them, and re-layouts  19.5 us (3%)
  between operations  13.4 us (2%)
    psum x2, waiting for transfers between devices, per_device(): gram_total = lax.psum(lax.psum(gram_part, 'aux'), 'orb') + identity_pad  135 us
    another operation x10, other arithmetic, per_device(): cholesky_low = jnp.linalg.cholesky(gram_total)  133 us
    all_gather x1, waiting for transfers between devices, per_device(): lax.all_gather(coeffs, 'aux', axis=1, tiled=True)  120 us
    another operation x5, other arithmetic, per_device(): lax.linalg.triangular_solve(cholesky_low, initial.astype(jnp.float32), le...  80.7 us
    reduce_scatter x1, waiting for transfers between devices, per_device(): lax.psum_scatter(partial_value, 'orb', scatter_dimension=1, tiled=True)  57.5 us
    reduce_scatter x1, waiting for transfers between devices, per_device(): lax.psum_scatter(picked, 'frag', scatter_dimension=0, tiled=True)  40.2 us
    dot_general x1, matrix products, per_device(): jnp.einsum('fmk,mq->fkq', lax.all_gather(coeffs, 'aux', axis=1, tiled=Tru...  23.5 us
  transfers between devices with their start and end apart: 5, of which 5 were waited for; matrix products, arithmetic and copies ran while one was open for 0% of the time, Pallas kernels for 0%

profile of v1, /device:TPU:1, one launch (start us, length us, event | category | flops | bytes accessed | tf_op | source)
XLA Modules:
  0.0 639.5 jit_solution(6426710730251401105)
XLA Ops:
  6.5 0.0 reduce-scatter.3.cloned.1.call-start
  6.5 0.7 compare_and_fusion
  7.3 10.3 %gather_fusion = bf16[2048,512]{1,0:T(8,128)(2,1)S(1)} fusion(bf16[4096,512]{1,0:T(8,128)(2,1)} %bitcast.50, s32[2048]{0:T(1024)S(1)} %broadcast_clamp_fusion), kind=kCustom, calls=%fused_computation | custom fusion | bytes 4202496 | tf_op jit(solution)/shard_map/jit(_take)/gather | solution.py:18
  17.6 2.4 copy.24
  20.0 3.2 select_select_fusion
  23.2 0.0 copy-start.5
  23.2 0.0 copy-start.6
  23.2 0.0 copy-start.4
  23.2 0.0 reduce-scatter.3.cloned.1.call-update
  23.2 0.0 all-reduce.4.cloned.1.call-start
  23.3 0.6 copy-done.5
  23.8 0.1 dynamic_slice.6
  23.9 0.0 copy-done.6
  23.9 0.1 dynamic_slice.7
  24.0 0.1 iota_compare_fusion.4
  24.1 0.2 copy-done.4
  24.3 0.0 copy-start.2
  24.3 40.2 %reduce-scatter.3.cloned.1.call-done = bf16[4,128,512]{1,2,0:T(8,128)(2,1)} async-done(((bf16[16,128,512]{1,2,0:T(8,128)(2,1)}), bf16[4,128,512]{1,2,0:T(8,128)(2,1)}) %reduce-scatter.3.cloned.1.call-update) | async-done | bytes 524304 | tf_op jit(solution)/shard_map/reduce_scatter | solution.py:22
  64.5 1.1 fusion.8
  65.6 1.5 fusion.2
  67.1 0.0 all-reduce.4.cloned.1.call-update
  67.1 0.0 copy-done.2
  67.1 0.0 all-reduce.6.cloned.1.call-start
  67.2 86.2 %all-reduce.4.cloned.1.call-done = f32[4,256,256]{1,2,0:T(8,128)} async-done(((f32[4,256,256]{1,2,0:T(8,128)}), f32[4,256,256]{1,2,0:T(8,128)}) %all-reduce.4.cloned.1.call-update) | async-done | bytes 1048592 | tf_op jit(solution)/shard_map/psum | solution.py:39
  153.4 0.0 all-reduce.6.cloned.1.call-update
  153.4 0.2 all-gather.2.cloned.1.call-start
  153.8 49.2 %all-reduce.6.cloned.1.call-done = f32[4,256,256]{1,2,0:T(8,128)} async-done(((f32[4,256,256]{1,2,0:T(8,128)}), f32[4,256,256]{1,2,0:T(8,128)}) %all-reduce.6.cloned.1.call-update) | async-done | bytes 1048592 | tf_op jit(solution)/shard_map/psum | solution.py:39
  203.0 0.0 copy-start
  203.0 1.4 multiply_add_fusion
  204.5 0.3 copy.27
  204.8 0.0 copy-done
  204.8 0.2 fusion.6
  205.0 46.9 %custom-call.16 = f32[4,128,128]{2,1,0:T(8,128)S(1)} custom-call(f32[4,128,128]{2,1,0:T(8,128)S(1)} %cholesky.122), custom_call_target="Cholesky" | custom-call | tf_op jit(solution)/shard_map/jit(cholesky)/cholesky | solution.py:40
  251.9 39.3 %custom-call.17 = f32[4,1,128,128]{2,3,1,0:T(8,128)S(1)} custom-call(f32[4,1,128,128]{3,2,1,0:T(8,128)S(1)} %select_bitcast_fusion), custom_call_target="InvertDiagBlocksLowerTriangular" | custom-call | tf_op jit(solution)/shard_map/jit(cholesky)/cholesky | solution.py:40
  291.3 0.1 cholesky.117
  291.4 0.4 constant_dynamic-update-slice_fusion.1
  291.8 0.7 convolution_subtract_fusion.1
  292.4 46.9 %custom-call.18 = f32[4,128,128]{2,1,0:T(8,128)S(1)} custom-call(f32[4,128,128]{2,1,0:T(8,128)S(1)} %convolution_subtract_fusion.1), custom_call_target="Cholesky" | custom-call | tf_op jit(solution)/shard_map/jit(cholesky)/cholesky | solution.py:40
  339.3 0.1 select_reduce_fusion
  339.4 0.1 compare_reduce_fusion
  339.5 0.1 compare_reduce_fusion.1
  339.6 0.0 copy-start.1
  339.6 0.2 select_select_fusion.1
  339.8 0.1 triangular_solve.63
  339.9 0.0 copy-start.3
  339.9 5.4 while.1
  339.9 0.6 fusion.25
  340.5 2.1 bitcast_dynamic-update-slice_fusion.2
  342.6 0.6 fusion.25
  343.2 2.1 bitcast_dynamic-update-slice_fusion.2
  345.3 79.4 %custom-call.19 = f32[4,2,128,128]{2,3,1,0:T(8,128)S(1)} custom-call(f32[4,2,128,128]{3,2,1,0:T(8,128)} %bitcast.54), custom_call_target="InvertDiagBlocksLowerTriangular" | custom-call | tf_op jit(solution)/shard_map/triangular_solve | solution.py:41
  424.7 0.0 copy-done.1
  424.7 0.6 fusion.18
  425.4 0.0 copy-done.3
  425.4 1.8 convolution_subtract_fusion
  427.2 1.1 convolution_convert_fusion
  428.3 1.0 pad_maximum_fusion
  429.3 0.0 all-gather.2.cloned.1.call-update
  429.4 0.0 reduce-scatter.5.cloned.1.call-start
  429.4 119.8 %all-gather.2.cloned.1.call-done = bf16[4,8192,256]{1,2,0:T(8,128)(2,1)} async-done(((bf16[4,512,256]{1,2,0:T(8,128)(2,1)}), bf16[4,8192,256]{1,2,0:T(8,128)(2,1)}) %all-gather.2.cloned.1.call-update) | async-done | bytes 16777232 | tf_op jit(solution)/shard_map/all_gather | solution.py:47
  549.2 23.5 %fusion = f32[4,256,1024]{2,1,0:T(8,128)} fusion(bf16[4,8192,256]{1,2,0:T(8,128)(2,1)} %all-gather.2.cloned.1.call-done, bf16[8192,1024]{1,0:T(8,128)(2,1)} %param.8), kind=kOutput, calls=%fused_computation.3 | convolution fusion | flops 17179869184 | bytes 37748736 | tf_op jit(solution)/shard_map/fmk,mq->fkq/dot_general | solution.py:45
  572.7 0.0 reduce-scatter.5.cloned.1.call-update
  572.8 57.5 %reduce-scatter.5.cloned.1.call-done = f32[4,128,1024]{2,1,0:T(8,128)} async-done(((f32[4,256,1024]{2,1,0:T(8,128)}), f32[4,128,1024]{2,1,0:T(8,128)}) %reduce-scatter.5.cloned.1.call-update) | async-done | bytes 2097168 | tf_op jit(solution)/shard_map/reduce_scatter | solution.py:51
  630.3 2.7 convert_element_type.23
  (15 shorter events, 0.2 us)
Async XLA Ops:
  6.5 58.0 %reduce-scatter.3.cloned.1.call-start = ((), (), s32[]{:S(2)}) async-start(), calls=%async_computation.2 | async-start | bytes 2621440 | tf_op jit(solution)/shard_map/reduce_scatter | solution.py:22
  23.2 0.7 copy-start.5
  23.2 0.7 copy-start.6
  23.2 1.1 copy-start.4
  23.2 130.2 %all-reduce.4.cloned.1.call-start = ((), (), s32[]{:S(2)}) async-start(), calls=%async_computation.3 | async-start | bytes 2097152 | tf_op jit(solution)/shard_map/psum | solution.py:39
  24.3 42.8 %copy-start.2 = (bf16[4,512,128]{2,1,0:T(8,128)(2,1)}, bf16[4,512,128]{2,1,0:T(8,128)(2,1)S(1)}, u32[]{:S(2)}) copy-start(bf16[4,512,128]{2,1,0:T(8,128)(2,1)S(1)} %bitcast_select_fusion) | copy-start | bytes 1572868
  67.1 135.9 %all-reduce.6.cloned.1.call-start = ((), (), s32[]{:S(2)}) async-start(), calls=%async_computation.4 | async-start | bytes 2097152 | tf_op jit(solution)/shard_map/psum | solution.py:39
  153.4 395.8 %all-gather.2.cloned.1.call-start = ((), (), s32[]{:S(2)}) async-start(), calls=%async_computation.5 | async-start | bytes 17825792 | tf_op jit(solution)/shard_map/all_gather | solution.py:47
  203.0 1.8 copy-start
  339.6 85.1 %copy-start.1 = (bf16[4,128,512]{1,2,0:T(8,128)(2,1)S(1)}, bf16[4,128,512]{1,2,0:T(8,128)(2,1)}, u32[]{:S(2)}) copy-start(bf16[4,128,512]{1,2,0:T(8,128)(2,1)} %reduce-scatter.3.cloned.1.call-done) | copy-start | bytes 1572868
  339.9 85.5 %copy-start.3 = (bf16[4,512,128]{2,1,0:T(8,128)(2,1)S(1)}, bf16[4,512,128]{2,1,0:T(8,128)(2,1)}, u32[]{:S(2)}) copy-start(bf16[4,512,128]{2,1,0:T(8,128)(2,1)} %copy-done.2) | copy-start | bytes 1572868
  429.4 200.9 %reduce-scatter.5.cloned.1.call-start = ((), (), s32[]{:S(2)}) async-start(), calls=%async_computation.6 | async-start | bytes 6291456 | tf_op jit(solution)/shard_map/reduce_scatter | solution.py:51
Sparse Core Ops, SparseCore 0:
  23.3 41.1 reduce-scatter.2
  67.8 85.5 all-reduce.3
  155.9 47.1 all-reduce.5
  429.5 119.7 all-gather.1
  572.9 57.3 reduce-scatter.4
